TPU v7x, 32 devices: a whole 2x2x4 slice. The times are simulated.
32 devices in a mesh: group: 2 (over x), trade: 16 (over z, y, core).
Axes of the slice: x: 2, y: 2, z: 4, core: 2. Of those that a mesh axis runs over, the one named last changes fastest.
Arguments:
- factors: bfloat16 [128, 128], P(('group', 'trade')), parts along dimension 0, may hold values from -6 to 6
- loadings: float32 [32, 16], replicated, may hold values from -1.5 to 1.5
- trade_coef: bfloat16 [65536, 256], P(('group', 'trade')), parts along dimension 0, may hold values from -0.75 to 0.75
- basis_size: int32 [65536], P(('group', 'trade')), parts along dimension 0, may hold values from 4 to 32
- set_ids: int32 [65536], P(('group', 'trade')), parts along dimension 0, may hold values from 0 to 31
- live_count: int32 [32], P(('group', 'trade')), parts along dimension 0, may hold values from 1 to 2047, as said below
- netting_row: int32 [64], P('group'), parts along dimension 0, may hold values from 0 to 31, each once
- threshold: float32 [64], P(('group', 'trade')), parts along dimension 0, may hold values from 0.5 to 8
- margin_start: float32 [64, 64], P(('group', 'trade')), parts along dimension 0, may hold values from 0 to 3
Outputs:
- expected: float32 [64, 8], P(('group', 'trade')), parts along dimension 0
There are 2 independent parts, one for each index of `group`. A program takes and returns all parts, laid end to end along the dimension named above; an argument that names none is the same for every part. Nothing has to cross between parts.
Inputs may be any that keep to these rules, and one draw needn't show every extreme that they name: `live_count`: blocks b and b + 8 hold exactly 2048 live trades together.
All inputs are finite; a program needn't handle non-finite values.
Results may differ from a plain program's by a relative error of at most 0.00035.
Values may be sent and summed in bfloat16 or wider, within the bound.
A program may use at most 64 MiB of HBM per device.

v0:
```python
import functools

import jax
import jax.numpy as jnp
from jax import lax
from jax.experimental import pallas as pl
from jax.experimental.pallas import tpu as pltpu
from jax.sharding import PartitionSpec as P

F = 16
K = 32
DATES = 8
LAG = 2
LANES = 128
CHUNK = 256
COLS = 512
MESH = pl.DeviceIdType.MESH
f32 = jnp.float32
bf16 = jnp.bfloat16


def iota(shape, axis):
    return lax.broadcasted_iota(jnp.int32, shape, axis)


def kernel(
    n,
    factors,
    loadings,
    trade_coef,
    basis_size,
    set_ids,
    live_count,
    netting_row,
    threshold,
    margin_start,
    out,
    fact,
    load_v,
    coef_v,
    size_v,
    ids_v,
    nrow_v,
    thr_s,
    marg_v,
    split,
    onehot,
    spread,
    basis,
    held,
    acc,
    part,
    recv,
    in_sem,
    gs_sem,
    gr_sem,
    ss_sem,
    sr_sem,
):
    me = lax.axis_index("trade")
    rows = fact.shape[1]
    near = n // 2
    paths = near * rows
    rep = max(1, LANES // paths)
    width = rep * paths
    slots = coef_v.shape[0]
    owned = recv.shape[2]
    mine = lax.div(me, near)
    sets = n * owned

    def each_peer(step, last_first=False):
        def at(i):
            i = n - 2 - i if last_first else i
            step(jnp.where(i >= me, i + 1, i))

        if n <= LANES // 4:
            for i in range(n - 1):
                at(i)
        else:
            lax.fori_loop(0, n - 1, lambda i, c: (at(i), c)[1], 0)

    def local(src, dst, i):
        return pltpu.make_async_copy(src, dst, in_sem.at[i])

    def settle(ref, sem, count):
        rest = ref.at[pl.ds(0, count)]
        pltpu.make_async_copy(rest, rest, sem).wait()

    barrier = pltpu.get_barrier_semaphore()
    each_peer(lambda j: pl.semaphore_signal(barrier, inc=1, device_id={"trade": j}, device_id_type=MESH))

    own = local(factors, fact.at[me], 0)
    limit_copy = local(threshold, thr_s, 1)
    pairs = (
        (loadings, load_v),
        (basis_size, size_v),
        (netting_row, nrow_v),
        (set_ids, ids_v),
        (margin_start, marg_v),
        (trade_coef, coef_v),
    )
    copies = [local(src, dst, 2) for src, dst in pairs]
    for copy in (own, *copies, limit_copy):
        copy.start()
    own.wait()
    pl.semaphore_wait(barrier, n - 1)

    def gather(j):
        return pltpu.make_async_remote_copy(
            src_ref=fact.at[me],
            dst_ref=fact.at[me],
            send_sem=gs_sem,
            recv_sem=gr_sem.at[mine],
            device_id={"trade": j},
            device_id_type=MESH,
        )

    each_peer(lambda j: gather(j).start(), last_first=True)

    for copy in copies:
        copy.wait()
    limit_copy.wait()
    tiled = (iota((F, LANES), 1) % F == iota((F, LANES), 0)).astype(f32).astype(bf16)
    diag = iota((DATES * K, LANES), 0) // K == iota((DATES * K, LANES), 1) // F
    rest = load_v[...]
    for i in range(3):
        piece = rest.astype(bf16)
        rest = rest - piece.astype(f32)
        wide = lax.dot_general(piece, tiled, (((0,), (0,)), ((), ())), preferred_element_type=f32)
        wide = jnp.concatenate([wide] * DATES, axis=0)
        split[i] = jnp.where(diag, wide, 0.0).astype(bf16)
    basis[...] = jnp.zeros(basis.shape, bf16)

    found = nrow_v[...] == iota((sets, sets), 0)
    owner_set = jnp.sum(jnp.where(found, iota((sets, sets), 1), 0).astype(f32), axis=1, keepdims=True)
    owner_set = owner_set.astype(jnp.int32)
    for c in range(slots // CHUNK):
        cut = slice(c * CHUNK, (c + 1) * CHUNK)
        onehot[:, cut] = (ids_v[:, cut] == owner_set).astype(f32).astype(bf16)

    for half in range(2):
        for i in range(LAG):
            held[half, :, i * paths : (i + 1) * paths] = marg_v[:, half * paths : (half + 1) * paths]

    live_now = live_count[0]
    slot_index = iota(size_v.shape, 0) * LANES + iota(size_v.shape, 1)
    used = jnp.where(slot_index < live_now, size_v[...], 0).astype(f32)
    basis_index = (iota((LANES, LANES), 1) % K).astype(f32)
    for c in range(slots // LANES):
        limit = jnp.broadcast_to(used[c : c + 1], (LANES, LANES)).T
        keep = basis_index < limit
        cut = slice(c * LANES, (c + 1) * LANES)
        for h in range(0, DATES * K, LANES):
            side = slice(h, h + LANES)
            coef_v[cut, side] = jnp.where(keep, coef_v[cut, side].astype(f32), 0.0).astype(bf16)

    def half_sums(half):
        for j in range(near):
            block = fact[half * near + j].astype(f32)
            for i in range(rep):
                at = i * paths + j * rows
                spread[at : at + rows] = block
        table = spread[...].astype(bf16)
        dims = (((1,), (1,)), ((), ()))
        loaded = lax.dot_general(split[2], table, dims, preferred_element_type=f32)
        loaded += lax.dot_general(split[1], table, dims, preferred_element_type=f32)
        loaded += lax.dot_general(split[0], table, dims, preferred_element_type=f32)
        bent = jnp.tanh(loaded)
        tall = rep * K
        pair = iota((tall, width), 0) // K == iota((tall, width), 1) // paths
        for j in range(DATES // rep):
            strip = jnp.where(pair, bent[j * tall : (j + 1) * tall], 0.0).astype(bf16)
            basis[j * tall : (j + 1) * tall, j * width : (j + 1) * width] = strip

        def block_sums(right):
            total = None
            for c in range(slots // CHUNK):
                cut = slice(c * CHUNK, (c + 1) * CHUNK)
                values = jnp.dot(coef_v[cut], right, preferred_element_type=f32).astype(bf16)
                term = jnp.dot(onehot[:, cut], values, preferred_element_type=f32)
                total = term if total is None else total + term
            return total

        blocks = max(1, acc.shape[1] // COLS)
        if blocks == 1:
            acc[...] = block_sums(basis[...])
        else:

            def one(b, carry):
                side = pl.ds(pl.multiple_of(b * COLS, COLS), COLS)
                acc[:, side] = block_sums(basis[:, side])
                return carry

            lax.fori_loop(0, blocks, one, 0)
        for j in range(n):
            part[half, j] = acc[j * owned : (j + 1) * owned]

    def scatter(j, half, stage):
        return pltpu.make_async_remote_copy(
            src_ref=part.at[half, j],
            dst_ref=recv.at[half, me],
            send_sem=ss_sem.at[stage],
            recv_sem=sr_sem.at[half],
            device_id={"trade": j},
            device_id_type=MESH,
        )

    settle(fact, gr_sem.at[mine], near - 1)
    half_sums(mine)
    each_peer(lambda j: scatter(j, mine, 0).start())
    settle(fact, gr_sem.at[1 - mine], near)
    half_sums(1 - mine)
    each_peer(lambda j: scatter(j, 1 - mine, 1).start())
    for half in range(2):
        recv[half, me] = part[half, me]
    settle(recv.at[0], sr_sem.at[0], n - 1)
    settle(recv.at[1], sr_sem.at[1], n - 1)

    row_at = iota((owned, 1), 0)
    limits = jnp.zeros((owned, 1), f32)
    for r in range(owned):
        limits = jnp.where(row_at == r, thr_s[r], limits)
    first = LAG * paths
    result = jnp.zeros(out.shape, f32)
    lane_date = iota((owned, width), 1) // paths
    column = iota(out.shape, 1)
    short = jnp.zeros((owned, DATES * paths), f32)
    for half in range(2):
        netted = recv[half, 0]
        for j in range(1, n):
            netted = netted + recv[half, j]
        margin = jnp.maximum(netted[:, : (DATES - LAG) * paths] - limits, 0.0)
        collateral = jnp.concatenate([held[half], margin], axis=1)
        short = short + jnp.maximum(netted - collateral, 0.0)
    for j in range(DATES // rep):
        block = short[:, j * width : (j + 1) * width]
        for i in range(rep):
            own_date = jnp.where(lane_date == i, block, 0.0) if rep > 1 else block
            result = jnp.where(column == j * rep + i, jnp.sum(own_date, axis=1, keepdims=True), result)
    out[...] = result
    settle(fact, gs_sem, n - 1)
    settle(recv.at[0], ss_sem.at[0], n - 1)
    settle(recv.at[1], ss_sem.at[1], n - 1)


def stay(x):
    return pltpu.with_memory_space_constraint(x, pltpu.MemorySpace.HBM)


def body(n, factors, loadings, trade_coef, basis_size, set_ids, live_count, netting_row, threshold, margin_start):
    rows = factors.shape[0]
    paths = n * rows
    half = paths // 2
    rep = max(1, LANES // half)
    slots = trade_coef.shape[0]
    sets = netting_row.shape[0]
    owned = threshold.shape[0]
    wide = DATES * half
    hbm = pl.BlockSpec(memory_space=pltpu.MemorySpace.HBM)
    total = pl.pallas_call(
        functools.partial(kernel, n),
        out_shape=jax.ShapeDtypeStruct((owned, DATES), f32),
        in_specs=[hbm] * 5 + [pl.BlockSpec(memory_space=pltpu.SMEM)] + [hbm] * 3,
        out_specs=pl.BlockSpec(memory_space=pltpu.VMEM),
        scratch_shapes=[
            pltpu.VMEM((n, rows, DATES * F), bf16),
            pltpu.VMEM((F, K), f32),
            pltpu.VMEM((slots, DATES * K), bf16),
            pltpu.VMEM((slots // LANES, LANES), jnp.int32),
            pltpu.VMEM((1, slots), jnp.int32),
            pltpu.VMEM((1, sets), jnp.int32),
            pltpu.SMEM((owned,), f32),
            pltpu.VMEM((owned, paths), f32),
            pltpu.VMEM((3, DATES * K, DATES * F), bf16),
            pltpu.VMEM((sets, slots), bf16),
            pltpu.VMEM((rep * half, DATES * F), f32),
            pltpu.VMEM((DATES * K, wide), bf16),
            pltpu.VMEM((2, owned, LAG * half), f32),
            pltpu.VMEM((sets, wide), f32),
            pltpu.VMEM((2, n, owned, wide), f32),
            pltpu.VMEM((2, n, owned, wide), f32),
            pltpu.SemaphoreType.DMA((3,)),
            pltpu.SemaphoreType.DMA,
            pltpu.SemaphoreType.DMA((2,)),
            pltpu.SemaphoreType.DMA((2,)),
            pltpu.SemaphoreType.DMA((2,)),
        ],
        compiler_params=pltpu.CompilerParams(
            collective_id=0, has_side_effects=True, vmem_limit_bytes=48 * 2**20
        ),
    )(
        stay(factors),
        stay(loadings.T),
        stay(trade_coef),
        stay(basis_size.reshape(slots // LANES, LANES)),
        stay(set_ids.reshape(1, slots)),
        live_count,
        stay(netting_row.reshape(1, sets)),
        stay(threshold),
        stay(margin_start),
    )
    return total / paths


def solution(mesh):
    return jax.shard_map(
        functools.partial(body, mesh.shape["trade"]),
        mesh=mesh,
        in_specs=(
            P(("group", "trade"), None),
            P(),
            P(("group", "trade"), None),
            P(("group", "trade")),
            P(("group", "trade")),
            P(("group", "trade")),
            P("group"),
            P(("group", "trade")),
            P(("group", "trade"), None),
        ),
        out_specs=P(("group", "trade"), None),
        check_vma=False,
    )
```

profile of v0, /device:TPU:0, one launch (start us, length us, event | category | flops | bytes accessed | tf_op | source)
XLA Modules:
  0.0 16.5 jit_solution(17986282571291424721)
XLA Ops:
  0.7 15.3 %shard_map.91 = f32[2,8]{1,0:T(2,128)S(1)} custom-call(bf16[4,128]{1,0:T(4,128)(2,1)} %factors.1, f32[16,32]{1,0:T(8,128)} %bitcast.4, bf16[2048,256]{1,0:T(8,128)(2,1)} %trade_coef.1, s32[16,128]{1,0:T(8,128)} %bitcast.5, s32[1,2048]{1,0:T(1,128)} %bitcast.6, s32[1]{0:T(128)S(6)} %copy.10.live_count, s32[1,32]{1,0:T(1,128)} %bitcast.7, f32[2]{0:T(128)} %threshold.1, ...), custom_call_target="tpu_custom_call" | custom-call | tf_op jit(solution)/shard_map/pallas_call | solution.py:260
  15.9 0.6 %broadcast_multiply_fusion = f32[2,8]{1,0:T(2,128)} fusion(f32[2,8]{1,0:T(2,128)S(1)} %shard_map.91), kind=kLoop, calls=%fused_computation | loop fusion | flops 16 | bytes 128 | tf_op jit(solution)/shard_map/div | solution.py:302
where the time goes:
time: 16.6 us; the launch traced here: 16.5 us
  Pallas kernels  15.3 us (92%)
  between operations  0.66 us (4%)
  other arithmetic  0.56 us (3%)
    pallas_call x1, Pallas kernels, body(): pl.pallas_call(functools.partial(kernel, n), out_shape=jax.ShapeDtypeStru...  15.3 us
    div x1, other arithmetic, body(): return total / paths  0.56 us

commit v1 on v0

--- a/solution.py
+++ b/solution.py
@@ -68,16 +68,23 @@
     mine = lax.div(me, near)
     sets = n * owned
 
-    def each_peer(step, last_first=False):
+    quarter = n // 4
+    hub = quarter + 1
+    is_hub = me == hub
+    is_late = me >= near
+    is_first = me < quarter
+    is_second = jnp.logical_and(jnp.logical_and(me >= quarter, me < near), me != hub)
+
+    def each(step, lo, hi, among=True):
         def at(i):
-            i = n - 2 - i if last_first else i
-            step(jnp.where(i >= me, i + 1, i))
-
+            step(jnp.where(i >= me, i + 1, i) if among else i)
+
+        count = hi - lo - 1 if among else hi - lo
         if n <= LANES // 4:
-            for i in range(n - 1):
+            for i in range(lo, lo + count):
                 at(i)
         else:
-            lax.fori_loop(0, n - 1, lambda i, c: (at(i), c)[1], 0)
+            lax.fori_loop(lo, lo + count, lambda i, c: (at(i), c)[1], 0)
 
     def local(src, dst, i):
         return pltpu.make_async_copy(src, dst, in_sem.at[i])
@@ -87,7 +94,22 @@
         pltpu.make_async_copy(rest, rest, sem).wait()
 
     barrier = pltpu.get_barrier_semaphore()
-    each_peer(lambda j: pl.semaphore_signal(barrier, inc=1, device_id={"trade": j}, device_id_type=MESH))
+
+    def greet(j):
+        pl.semaphore_signal(barrier, inc=1, device_id={"trade": j}, device_id_type=MESH)
+
+    @pl.when(jnp.logical_or(is_first, is_hub))
+    def _():
+        each(greet, 0, n)
+
+    @pl.when(is_second)
+    def _():
+        each(greet, quarter, n)
+
+    @pl.when(is_late)
+    def _():
+        greet(hub)
+        each(greet, near, n)
 
     own = local(factors, fact.at[me], 0)
     limit_copy = local(threshold, thr_s, 1)
@@ -103,7 +125,6 @@
     for copy in (own, *copies, limit_copy):
         copy.start()
     own.wait()
-    pl.semaphore_wait(barrier, n - 1)
 
     def gather(j):
         return pltpu.make_async_remote_copy(
@@ -115,7 +136,36 @@
             device_id_type=MESH,
         )
 
-    each_peer(lambda j: gather(j).start(), last_first=True)
+    def relay(j, count):
+        return pltpu.make_async_remote_copy(
+            src_ref=fact.at[pl.ds(0, count)],
+            dst_ref=fact.at[pl.ds(0, count)],
+            send_sem=gs_sem,
+            recv_sem=gr_sem.at[0],
+            device_id={"trade": j},
+            device_id_type=MESH,
+        )
+
+    @pl.when(is_first)
+    def _():
+        pl.semaphore_wait(barrier, quarter)
+        gather(hub).start()
+        each(lambda j: gather(j).start(), 0, quarter)
+
+    @pl.when(is_second)
+    def _():
+        pl.semaphore_wait(barrier, near - 1)
+        each(lambda j: gather(j).start(), 0, near)
+
+    @pl.when(is_hub)
+    def _():
+        pl.semaphore_wait(barrier, n - 1)
+        each(lambda j: gather(j).start(), 0, near)
+
+    @pl.when(is_late)
+    def _():
+        pl.semaphore_wait(barrier, n - 1)
+        each(lambda j: gather(j).start(), 0, n)
 
     for copy in copies:
         copy.wait()
@@ -173,11 +223,11 @@
             basis[j * tall : (j + 1) * tall, j * width : (j + 1) * width] = strip
 
         def block_sums(right):
+            cuts = [slice(c * CHUNK, (c + 1) * CHUNK) for c in range(slots // CHUNK)]
+            values = [jnp.dot(coef_v[cut], right, preferred_element_type=f32).astype(bf16) for cut in cuts]
             total = None
-            for c in range(slots // CHUNK):
-                cut = slice(c * CHUNK, (c + 1) * CHUNK)
-                values = jnp.dot(coef_v[cut], right, preferred_element_type=f32).astype(bf16)
-                term = jnp.dot(onehot[:, cut], values, preferred_element_type=f32)
+            for cut, value in zip(cuts, values):
+                term = jnp.dot(onehot[:, cut], value, preferred_element_type=f32)
                 total = term if total is None else total + term
             return total
 
@@ -206,11 +256,30 @@
         )
 
     settle(fact, gr_sem.at[mine], near - 1)
+
+    @pl.when(is_hub)
+    def _():
+        each(lambda j: relay(j, near).start(), near, n, among=False)
+        each(lambda j: relay(j, quarter).start(), quarter, near)
+
     half_sums(mine)
-    each_peer(lambda j: scatter(j, mine, 0).start())
+
+    @pl.when(is_late)
+    def _():
+        each(lambda j: scatter(j, mine, 0).start(), 0, n)
+
+    @pl.when(jnp.logical_not(is_late))
+    def _():
+        each(lambda j: scatter(j, mine, 0).start(), 0, near)
+
     settle(fact, gr_sem.at[1 - mine], near)
+
+    @pl.when(jnp.logical_not(is_late))
+    def _():
+        each(lambda j: scatter(j, mine, 0).start(), near, n, among=False)
+
     half_sums(1 - mine)
-    each_peer(lambda j: scatter(j, 1 - mine, 1).start())
+    each(lambda j: scatter(j, 1 - mine, 1).start(), 0, n)
     for half in range(2):
         recv[half, me] = part[half, me]
     settle(recv.at[0], sr_sem.at[0], n - 1)
@@ -238,7 +307,24 @@
             own_date = jnp.where(lane_date == i, block, 0.0) if rep > 1 else block
             result = jnp.where(column == j * rep + i, jnp.sum(own_date, axis=1, keepdims=True), result)
     out[...] = result
-    settle(fact, gs_sem, n - 1)
+
+    @pl.when(is_first)
+    def _():
+        settle(fact, gs_sem, quarter)
+
+    @pl.when(jnp.logical_or(is_second, is_hub))
+    def _():
+        settle(fact, gs_sem, near - 1)
+
+    @pl.when(is_hub)
+    def _():
+        each(lambda j: settle(fact, gs_sem, near), near, n, among=False)
+        each(lambda j: settle(fact, gs_sem, quarter), quarter, near)
+
+    @pl.when(is_late)
+    def _():
+        settle(fact, gs_sem, n - 1)
+
     settle(recv.at[0], ss_sem.at[0], n - 1)
     settle(recv.at[1], ss_sem.at[1], n - 1)
 

time: 16.6 us -> 16.1 us (0.970)
  Pallas kernels: 15.3 us -> 14.7 us
    pallas_call x1, Pallas kernels: 15.3 us -> 14.7 us  [body(): pl.pallas_call(functools.partial(kernel, n), out_shape=jax.ShapeDtypeStru...]
where the time goes in v1:
time: 16.1 us; the launch traced here: 15.9 us
  Pallas kernels  14.7 us (91%)
  between operations  0.66 us (4%)
  other arithmetic  0.56 us (3%)
    pallas_call x1, Pallas kernels, body(): pl.pallas_call(functools.partial(kernel, n), out_shape=jax.ShapeDtypeStru...  14.7 us
    div x1, other arithmetic, body(): return total / paths  0.56 us

profile of v1, /device:TPU:0, one launch (start us, length us, event | category | flops | bytes accessed | tf_op | source)
XLA Modules:
  0.0 15.9 jit_solution(16119040084797266881)
XLA Ops:
  0.7 14.7 %shard_map.91 = f32[2,8]{1,0:T(2,128)S(1)} custom-call(bf16[4,128]{1,0:T(4,128)(2,1)} %factors.1, f32[16,32]{1,0:T(8,128)} %bitcast.4, bf16[2048,256]{1,0:T(8,128)(2,1)} %trade_coef.1, s32[16,128]{1,0:T(8,128)} %bitcast.5, s32[1,2048]{1,0:T(1,128)} %bitcast.6, s32[1]{0:T(128)S(6)} %copy.10.live_count, s32[1,32]{1,0:T(1,128)} %bitcast.7, f32[2]{0:T(128)} %threshold.1, ...), custom_call_target="tpu_custom_call" | custom-call | tf_op jit(solution)/shard_map/pallas_call | solution.py:346
  15.3 0.6 %broadcast_multiply_fusion = f32[2,8]{1,0:T(2,128)} fusion(f32[2,8]{1,0:T(2,128)S(1)} %shard_map.91), kind=kLoop, calls=%fused_computation | loop fusion | flops 16 | bytes 128 | tf_op jit(solution)/shard_map/div | solution.py:388

commit v2 on v1

--- a/solution.py
+++ b/solution.py
@@ -49,6 +49,7 @@
     basis,
     held,
     acc,
+    pooled,
     part,
     recv,
     in_sem,
@@ -72,6 +73,7 @@
     hub = quarter + 1
     is_hub = me == hub
     is_late = me >= near
+    is_last = me >= n - quarter
     is_first = me < quarter
     is_second = jnp.logical_and(jnp.logical_and(me >= quarter, me < near), me != hub)
 
@@ -204,7 +206,19 @@
             side = slice(h, h + LANES)
             coef_v[cut, side] = jnp.where(keep, coef_v[cut, side].astype(f32), 0.0).astype(bf16)
 
-    def half_sums(half):
+    @pl.when(is_last)
+    def _():
+        rest = None
+        for c in range(slots // CHUNK):
+            cut = slice(c * CHUNK, (c + 1) * CHUNK)
+            term = jnp.dot(onehot[:, cut], coef_v[cut], preferred_element_type=f32)
+            rest = term if rest is None else rest + term
+        for i in range(3):
+            piece = rest.astype(bf16)
+            rest = rest - piece.astype(f32)
+            pooled[i * sets : (i + 1) * sets] = piece
+
+    def half_sums(half, pool=False):
         for j in range(near):
             block = fact[half * near + j].astype(f32)
             for i in range(rep):
@@ -223,6 +237,9 @@
             basis[j * tall : (j + 1) * tall, j * width : (j + 1) * width] = strip
 
         def block_sums(right):
+            if pool:
+                thirds = jnp.dot(pooled[...], right, preferred_element_type=f32)
+                return thirds[2 * sets :] + thirds[sets : 2 * sets] + thirds[:sets]
             cuts = [slice(c * CHUNK, (c + 1) * CHUNK) for c in range(slots // CHUNK)]
             values = [jnp.dot(coef_v[cut], right, preferred_element_type=f32).astype(bf16) for cut in cuts]
             total = None
@@ -259,7 +276,7 @@
 
     @pl.when(is_hub)
     def _():
-        each(lambda j: relay(j, near).start(), near, n, among=False)
+        each(lambda i: relay(n - 1 - i, near).start(), 0, near, among=False)
         each(lambda j: relay(j, quarter).start(), quarter, near)
 
     half_sums(mine)
@@ -278,7 +295,15 @@
     def _():
         each(lambda j: scatter(j, mine, 0).start(), near, n, among=False)
 
-    half_sums(1 - mine)
+
+    @pl.when(is_last)
+    def _():
+        half_sums(1 - mine, pool=True)
+
+    @pl.when(jnp.logical_not(is_last))
+    def _():
+        half_sums(1 - mine)
+
     each(lambda j: scatter(j, 1 - mine, 1).start(), 0, n)
     for half in range(2):
         recv[half, me] = part[half, me]
@@ -363,6 +388,7 @@
             pltpu.VMEM((DATES * K, wide), bf16),
             pltpu.VMEM((2, owned, LAG * half), f32),
             pltpu.VMEM((sets, wide), f32),
+            pltpu.VMEM((3 * sets, DATES * K), bf16),
             pltpu.VMEM((2, n, owned, wide), f32),
             pltpu.VMEM((2, n, owned, wide), f32),
             pltpu.SemaphoreType.DMA((3,)),

time: 16.1 us -> 15.3 us (0.950)
  Pallas kernels: 14.7 us -> 13.9 us
    pallas_call x1, Pallas kernels: 14.7 us -> 13.9 us  [body(): pl.pallas_call(functools.partial(kernel, n), out_shape=jax.ShapeDtypeStru...]
where the time goes in v2:
time: 15.3 us; the launch traced here: 15.1 us
  Pallas kernels  13.9 us (91%)
  between operations  0.66 us (4%)
  other arithmetic  0.56 us (4%)
    pallas_call x1, Pallas kernels, body(): pl.pallas_call(functools.partial(kernel, n), out_shape=jax.ShapeDtypeStru...  13.9 us
    div x1, other arithmetic, body(): return total / paths  0.56 us

profile of v2, /device:TPU:0, one launch (start us, length us, event | category | flops | bytes accessed | tf_op | source)
XLA Modules:
  0.0 15.1 jit_solution(14993597900504177351)
XLA Ops:
  0.7 13.9 %shard_map.91 = f32[2,8]{1,0:T(2,128)S(1)} custom-call(bf16[4,128]{1,0:T(4,128)(2,1)} %factors.1, f32[16,32]{1,0:T(8,128)} %bitcast.4, bf16[2048,256]{1,0:T(8,128)(2,1)} %trade_coef.1, s32[16,128]{1,0:T(8,128)} %bitcast.5, s32[1,2048]{1,0:T(1,128)} %bitcast.6, s32[1]{0:T(128)S(6)} %copy.10.live_count, s32[1,32]{1,0:T(1,128)} %bitcast.7, f32[2]{0:T(128)} %threshold.1, ...), custom_call_target="tpu_custom_call" | custom-call | tf_op jit(solution)/shard_map/pallas_call | solution.py:371
  14.6 0.6 %broadcast_multiply_fusion = f32[2,8]{1,0:T(2,128)} fusion(f32[2,8]{1,0:T(2,128)S(1)} %shard_map.91), kind=kLoop, calls=%fused_computation | loop fusion | flops 16 | bytes 128 | tf_op jit(solution)/shard_map/div | solution.py:414

commit v3 on v1

--- a/solution.py
+++ b/solution.py
@@ -51,11 +51,17 @@
     acc,
     part,
     recv,
+    part_c,
+    recv_c,
     in_sem,
     gs_sem,
     gr_sem,
+    pair_sem,
     ss_sem,
     sr_sem,
+    cs_sem,
+    cr_sem,
+    ready,
 ):
     me = lax.axis_index("trade")
     rows = fact.shape[1]
@@ -72,8 +78,13 @@
     hub = quarter + 1
     is_hub = me == hub
     is_late = me >= near
-    is_first = me < quarter
-    is_second = jnp.logical_and(jnp.logical_and(me >= quarter, me < near), me != hub)
+    last = n - quarter
+    odd = lax.rem(me, 2) == 1
+    is_last = me >= last
+    is_even = jnp.logical_and(jnp.logical_and(is_late, me < last), jnp.logical_not(odd))
+    is_odd = jnp.logical_and(jnp.logical_and(is_late, me < last), odd)
+    pool = n - recv_c.shape[0]
+    is_early = jnp.logical_not(is_late)
 
     def each(step, lo, hi, among=True):
         def at(i):
@@ -98,18 +109,20 @@
     def greet(j):
         pl.semaphore_signal(barrier, inc=1, device_id={"trade": j}, device_id_type=MESH)
 
-    @pl.when(jnp.logical_or(is_first, is_hub))
+    @pl.when(is_early)
     def _():
         each(greet, 0, n)
 
-    @pl.when(is_second)
-    def _():
-        each(greet, quarter, n)
-
-    @pl.when(is_late)
+    @pl.when(jnp.logical_or(is_even, is_odd))
     def _():
         greet(hub)
         each(greet, near, n)
+
+    @pl.when(is_last)
+    def _():
+        greet(hub)
+        each(lambda i: greet(near + 1 + 2 * i), 0, quarter // 2, among=False)
+        each(greet, last, n)
 
     own = local(factors, fact.at[me], 0)
     limit_copy = local(threshold, thr_s, 1)
@@ -136,33 +149,71 @@
             device_id_type=MESH,
         )
 
-    def relay(j, count):
+    def relay(j):
         return pltpu.make_async_remote_copy(
-            src_ref=fact.at[pl.ds(0, count)],
-            dst_ref=fact.at[pl.ds(0, count)],
+            src_ref=fact.at[pl.ds(0, near)],
+            dst_ref=fact.at[pl.ds(0, near)],
             send_sem=gs_sem,
             recv_sem=gr_sem.at[0],
             device_id={"trade": j},
             device_id_type=MESH,
         )
 
-    @pl.when(is_first)
-    def _():
-        pl.semaphore_wait(barrier, quarter)
-        gather(hub).start()
-        each(lambda j: gather(j).start(), 0, quarter)
-
-    @pl.when(is_second)
+    def report():
+        pl.semaphore_signal(ready, inc=1, device_id={"trade": hub}, device_id_type=MESH)
+
+    @pl.when(jnp.logical_and(is_early, me != hub))
     def _():
         pl.semaphore_wait(barrier, near - 1)
+        report()
         each(lambda j: gather(j).start(), 0, near)
 
     @pl.when(is_hub)
     def _():
+        pl.semaphore_wait(ready, near - 1)
+        each(lambda j: gather(j).start(), 0, near)
+
+    def to_partner():
+        return pltpu.make_async_remote_copy(
+            src_ref=fact.at[me],
+            dst_ref=fact.at[me],
+            send_sem=gs_sem,
+            recv_sem=pair_sem,
+            device_id={"trade": me + 1},
+            device_id_type=MESH,
+        )
+
+    def pair(j):
+        both = pl.ds(me - 1, 2)
+        return pltpu.make_async_remote_copy(
+            src_ref=fact.at[both],
+            dst_ref=fact.at[both],
+            send_sem=gs_sem,
+            recv_sem=gr_sem.at[1],
+            device_id={"trade": j},
+            device_id_type=MESH,
+        )
+
+    @pl.when(is_even)
+    def _():
+        pl.semaphore_wait(barrier, last - 1)
+        to_partner().start()
+
+        def send(j):
+            @pl.when(j != me + 1)
+            def _():
+                gather(j).start()
+
+        each(send, 0, last)
+
+    @pl.when(is_odd)
+    def _():
         pl.semaphore_wait(barrier, n - 1)
-        each(lambda j: gather(j).start(), 0, near)
-
-    @pl.when(is_late)
+        settle(fact, pair_sem, 1)
+        each(lambda i: pair(n - 1 - i).start(), 0, quarter, among=False)
+        each(lambda j: gather(j).start(), 0, last)
+
+    @pl.when(is_last)
     def _():
         pl.semaphore_wait(barrier, n - 1)
         each(lambda j: gather(j).start(), 0, n)
@@ -204,7 +255,29 @@
             side = slice(h, h + LANES)
             coef_v[cut, side] = jnp.where(keep, coef_v[cut, side].astype(f32), 0.0).astype(bf16)
 
-    def half_sums(half):
+    def pass_coefs(j):
+        return pltpu.make_async_remote_copy(
+            src_ref=part_c.at[j],
+            dst_ref=recv_c.at[me - pool],
+            send_sem=cs_sem,
+            recv_sem=cr_sem,
+            device_id={"trade": j},
+            device_id_type=MESH,
+        )
+
+    @pl.when(is_late)
+    def _():
+        total = None
+        for c in range(slots // CHUNK):
+            cut = slice(c * CHUNK, (c + 1) * CHUNK)
+            term = jnp.dot(onehot[:, cut], coef_v[cut], preferred_element_type=f32)
+            total = term if total is None else total + term
+        for j in range(n):
+            part_c[j] = total[j * owned : (j + 1) * owned]
+        each(lambda j: pass_coefs(j).start(), 0, near, among=False)
+        recv_c[me - pool] = part_c[me]
+
+    def make_basis(half):
         for j in range(near):
             block = fact[half * near + j].astype(f32)
             for i in range(rep):
@@ -220,7 +293,10 @@
         pair = iota((tall, width), 0) // K == iota((tall, width), 1) // paths
         for j in range(DATES // rep):
             strip = jnp.where(pair, bent[j * tall : (j + 1) * tall], 0.0).astype(bf16)
-            basis[j * tall : (j + 1) * tall, j * width : (j + 1) * width] = strip
+            basis[half, j * tall : (j + 1) * tall, j * width : (j + 1) * width] = strip
+
+    def half_sums(half):
+        make_basis(half)
 
         def block_sums(right):
             cuts = [slice(c * CHUNK, (c + 1) * CHUNK) for c in range(slots // CHUNK)]
@@ -233,12 +309,12 @@
 
         blocks = max(1, acc.shape[1] // COLS)
         if blocks == 1:
-            acc[...] = block_sums(basis[...])
+            acc[...] = block_sums(basis[half])
         else:
 
             def one(b, carry):
                 side = pl.ds(pl.multiple_of(b * COLS, COLS), COLS)
-                acc[:, side] = block_sums(basis[:, side])
+                acc[:, side] = block_sums(basis[half, :, side])
                 return carry
 
             lax.fori_loop(0, blocks, one, 0)
@@ -255,35 +331,64 @@
             device_id_type=MESH,
         )
 
-    settle(fact, gr_sem.at[mine], near - 1)
-
     @pl.when(is_hub)
     def _():
-        each(lambda j: relay(j, near).start(), near, n, among=False)
-        each(lambda j: relay(j, quarter).start(), quarter, near)
-
+        pl.semaphore_wait(barrier, n - 1)
+
+    @pl.when(is_odd)
+    def _():
+        settle(fact, gr_sem.at[1], near - 2)
+
+    @pl.when(jnp.logical_not(is_odd))
+    def _():
+        settle(fact, gr_sem.at[mine], near - 1)
+
+    @pl.when(is_hub)
+    def _():
+        each(lambda i: relay(n - 1 - i).start(), 0, near, among=False)
     half_sums(mine)
 
     @pl.when(is_late)
     def _():
         each(lambda j: scatter(j, mine, 0).start(), 0, n)
-
-    @pl.when(jnp.logical_not(is_late))
+        each(lambda j: pass_coefs(j).start(), near, n)
+
+    @pl.when(is_early)
     def _():
         each(lambda j: scatter(j, mine, 0).start(), 0, near)
 
     settle(fact, gr_sem.at[1 - mine], near)
 
-    @pl.when(jnp.logical_not(is_late))
+    @pl.when(is_early)
     def _():
         each(lambda j: scatter(j, mine, 0).start(), near, n, among=False)
 
-    half_sums(1 - mine)
-    each(lambda j: scatter(j, 1 - mine, 1).start(), 0, n)
-    for half in range(2):
-        recv[half, me] = part[half, me]
-    settle(recv.at[0], sr_sem.at[0], n - 1)
-    settle(recv.at[1], sr_sem.at[1], n - 1)
+
+    @pl.when(is_early)
+    def _():
+        half_sums(1 - mine)
+        each(lambda j: scatter(j, 1 - mine, 1).start(), 0, n)
+        recv[1 - mine, me] = part[1 - mine, me]
+        settle(recv_c, cr_sem, n - pool)
+
+    @pl.when(is_late)
+    def _():
+        make_basis(1 - mine)
+        settle(recv_c, cr_sem, n - pool - 1)
+
+    recv[mine, me] = part[mine, me]
+    rest = recv_c[0]
+    for j in range(1, n - pool):
+        rest = rest + recv_c[j]
+    pieces = []
+    for i in range(3):
+        pieces.append(rest.astype(bf16).astype(f32))
+        rest = rest - pieces[i]
+    stack = jnp.concatenate(pieces, axis=0).astype(bf16)
+    thirds = jnp.dot(stack, basis[0], preferred_element_type=f32)
+    recv[0, pool] = thirds[2 * owned :] + thirds[owned : 2 * owned] + thirds[:owned]
+    for j in range(pool + 1, n):
+        recv[0, j] = jnp.zeros(recv.shape[2:], f32)
 
     row_at = iota((owned, 1), 0)
     limits = jnp.zeros((owned, 1), f32)
@@ -293,14 +398,26 @@
     result = jnp.zeros(out.shape, f32)
     lane_date = iota((owned, width), 1) // paths
     column = iota(out.shape, 1)
-    short = jnp.zeros((owned, DATES * paths), f32)
-    for half in range(2):
+
+    def shortfall(half):
         netted = recv[half, 0]
         for j in range(1, n):
             netted = netted + recv[half, j]
         margin = jnp.maximum(netted[:, : (DATES - LAG) * paths] - limits, 0.0)
         collateral = jnp.concatenate([held[half], margin], axis=1)
-        short = short + jnp.maximum(netted - collateral, 0.0)
+        return jnp.maximum(netted - collateral, 0.0)
+
+    @pl.when(is_early)
+    def _():
+        settle(recv.at[0], sr_sem.at[0], pool - 1)
+
+    @pl.when(is_late)
+    def _():
+        settle(recv.at[0], sr_sem.at[0], pool)
+
+    short = shortfall(0)
+    settle(recv.at[1], sr_sem.at[1], n - 1)
+    short = short + shortfall(1)
     for j in range(DATES // rep):
         block = short[:, j * width : (j + 1) * width]
         for i in range(rep):
@@ -308,25 +425,35 @@
             result = jnp.where(column == j * rep + i, jnp.sum(own_date, axis=1, keepdims=True), result)
     out[...] = result
 
-    @pl.when(is_first)
-    def _():
-        settle(fact, gs_sem, quarter)
-
-    @pl.when(jnp.logical_or(is_second, is_hub))
+    @pl.when(is_early)
     def _():
         settle(fact, gs_sem, near - 1)
 
     @pl.when(is_hub)
     def _():
         each(lambda j: settle(fact, gs_sem, near), near, n, among=False)
-        each(lambda j: settle(fact, gs_sem, quarter), quarter, near)
+
+    @pl.when(jnp.logical_or(is_even, is_odd))
+    def _():
+        settle(fact, gs_sem, last - 1)
+
+    @pl.when(is_odd)
+    def _():
+        settle(fact, gs_sem, 2 * quarter)
+
+    @pl.when(is_last)
+    def _():
+        settle(fact, gs_sem, n - 1)
+
+    settle(recv.at[0], ss_sem.at[0], n - 1)
+
+    @pl.when(is_early)
+    def _():
+        settle(recv.at[1], ss_sem.at[1], n - 1)
 
     @pl.when(is_late)
     def _():
-        settle(fact, gs_sem, n - 1)
-
-    settle(recv.at[0], ss_sem.at[0], n - 1)
-    settle(recv.at[1], ss_sem.at[1], n - 1)
+        settle(part_c, cs_sem, n - 1)
 
 
 def stay(x):
@@ -360,16 +487,22 @@
             pltpu.VMEM((3, DATES * K, DATES * F), bf16),
             pltpu.VMEM((sets, slots), bf16),
             pltpu.VMEM((rep * half, DATES * F), f32),
-            pltpu.VMEM((DATES * K, wide), bf16),
+            pltpu.VMEM((2, DATES * K, wide), bf16),
             pltpu.VMEM((2, owned, LAG * half), f32),
             pltpu.VMEM((sets, wide), f32),
             pltpu.VMEM((2, n, owned, wide), f32),
             pltpu.VMEM((2, n, owned, wide), f32),
+            pltpu.VMEM((n, owned, DATES * K), f32),
+            pltpu.VMEM((n // 2, owned, DATES * K), f32),
             pltpu.SemaphoreType.DMA((3,)),
             pltpu.SemaphoreType.DMA,
             pltpu.SemaphoreType.DMA((2,)),
+            pltpu.SemaphoreType.DMA,
             pltpu.SemaphoreType.DMA((2,)),
             pltpu.SemaphoreType.DMA((2,)),
+            pltpu.SemaphoreType.DMA,
+            pltpu.SemaphoreType.DMA,
+            pltpu.SemaphoreType.REGULAR,
         ],
         compiler_params=pltpu.CompilerParams(
             collective_id=0, has_side_effects=True, vmem_limit_bytes=48 * 2**20

time: 16.1 us -> 14.2 us (0.88)
  Pallas kernels: 14.7 us -> 12.9 us
    pallas_call x1, Pallas kernels: 14.7 us -> 12.9 us  [body(): pl.pallas_call(functools.partial(kernel, n), out_shape=jax.ShapeDtypeStru...]
where the time goes in v3:
time: 14.2 us; the launch traced here: 14.1 us
  Pallas kernels  12.9 us (91%)
  between operations  0.66 us (5%)
  other arithmetic  0.56 us (4%)
    pallas_call x1, Pallas kernels, body(): pl.pallas_call(functools.partial(kernel, n), out_shape=jax.ShapeDtypeStru...  12.9 us
    div x1, other arithmetic, body(): return total / paths  0.56 us

profile of v3, /device:TPU:0, one launch (start us, length us, event | category | flops | bytes accessed | tf_op | source)
XLA Modules:
  0.0 14.1 jit_solution(15324809667284758586)
XLA Ops:
  0.7 12.9 %shard_map.91 = f32[2,8]{1,0:T(2,128)S(1)} custom-call(bf16[4,128]{1,0:T(4,128)(2,1)} %factors.1, f32[16,32]{1,0:T(8,128)} %bitcast.4, bf16[2048,256]{1,0:T(8,128)(2,1)} %trade_coef.1, s32[16,128]{1,0:T(8,128)} %bitcast.5, s32[1,2048]{1,0:T(1,128)} %bitcast.6, s32[1]{0:T(128)S(6)} %copy.10.live_count, s32[1,32]{1,0:T(1,128)} %bitcast.7, f32[2]{0:T(128)} %threshold.1, ...), custom_call_target="tpu_custom_call" | custom-call | tf_op jit(solution)/shard_map/pallas_call | solution.py:473
  13.5 0.6 %broadcast_multiply_fusion = f32[2,8]{1,0:T(2,128)} fusion(f32[2,8]{1,0:T(2,128)S(1)} %shard_map.91), kind=kLoop, calls=%fused_computation | loop fusion | flops 16 | bytes 128 | tf_op jit(solution)/shard_map/div | solution.py:521

commit v4 on v3

--- a/solution.py
+++ b/solution.py
@@ -78,11 +78,11 @@
     hub = quarter + 1
     is_hub = me == hub
     is_late = me >= near
-    last = n - quarter
+    slow = near + 1
     odd = lax.rem(me, 2) == 1
-    is_last = me >= last
-    is_even = jnp.logical_and(jnp.logical_and(is_late, me < last), jnp.logical_not(odd))
-    is_odd = jnp.logical_and(jnp.logical_and(is_late, me < last), odd)
+    is_even = jnp.logical_and(is_late, jnp.logical_not(odd))
+    is_odd = jnp.logical_and(is_late, odd)
+    is_final = me >= n - 2
     pool = n - recv_c.shape[0]
     is_early = jnp.logical_not(is_late)
 
@@ -111,18 +111,27 @@
 
     @pl.when(is_early)
     def _():
-        each(greet, 0, n)
-
-    @pl.when(jnp.logical_or(is_even, is_odd))
-    def _():
-        greet(hub)
-        each(greet, near, n)
-
-    @pl.when(is_last)
-    def _():
-        greet(hub)
-        each(lambda i: greet(near + 1 + 2 * i), 0, quarter // 2, among=False)
-        each(greet, last, n)
+        each(greet, 0, near)
+
+    def each_odd(step):
+        def at(i):
+            j = near + 1 + 2 * i
+
+            @pl.when(j != me)
+            def _():
+                step(j)
+
+        if n <= LANES // 4:
+            for i in range(quarter - 1, -1, -1):
+                at(i)
+        else:
+            lax.fori_loop(0, quarter, lambda i, c: (at(quarter - 1 - i), c)[1], 0)
+
+    @pl.when(is_odd)
+    def _():
+        greet(me - 1)
+
+    each_odd(greet)
 
     own = local(factors, fact.at[me], 0)
     limit_copy = local(threshold, thr_s, 1)
@@ -137,14 +146,12 @@
     copies = [local(src, dst, 2) for src, dst in pairs]
     for copy in (own, *copies, limit_copy):
         copy.start()
-    own.wait()
-
-    def gather(j):
+    def gather(j, lane=None):
         return pltpu.make_async_remote_copy(
             src_ref=fact.at[me],
             dst_ref=fact.at[me],
             send_sem=gs_sem,
-            recv_sem=gr_sem.at[mine],
+            recv_sem=gr_sem.at[mine if lane is None else lane],
             device_id={"trade": j},
             device_id_type=MESH,
         )
@@ -159,23 +166,15 @@
             device_id_type=MESH,
         )
 
-    def report():
-        pl.semaphore_signal(ready, inc=1, device_id={"trade": hub}, device_id_type=MESH)
-
-    @pl.when(jnp.logical_and(is_early, me != hub))
-    def _():
+    @pl.when(is_early)
+    def _():
+        own.wait()
         pl.semaphore_wait(barrier, near - 1)
-        report()
-        each(lambda j: gather(j).start(), 0, near)
-
-    @pl.when(is_hub)
-    def _():
-        pl.semaphore_wait(ready, near - 1)
         each(lambda j: gather(j).start(), 0, near)
 
     def to_partner():
         return pltpu.make_async_remote_copy(
-            src_ref=fact.at[me],
+            src_ref=factors,
             dst_ref=fact.at[me],
             send_sem=gs_sem,
             recv_sem=pair_sem,
@@ -189,34 +188,31 @@
             src_ref=fact.at[both],
             dst_ref=fact.at[both],
             send_sem=gs_sem,
-            recv_sem=gr_sem.at[1],
+            recv_sem=gr_sem.at[jnp.where(jnp.logical_and(me == slow, j >= n - 2), 2, 1)],
             device_id={"trade": j},
             device_id_type=MESH,
         )
 
     @pl.when(is_even)
     def _():
-        pl.semaphore_wait(barrier, last - 1)
+        pl.semaphore_wait(barrier, 1)
         to_partner().start()
-
-        def send(j):
-            @pl.when(j != me + 1)
-            def _():
-                gather(j).start()
-
-        each(send, 0, last)
+        own.wait()
 
     @pl.when(is_odd)
     def _():
+        own.wait()
         pl.semaphore_wait(barrier, n - 1)
+
+        @pl.when(me == slow)
+        def _():
+            pl.semaphore_signal(ready, inc=1, device_id={"trade": hub}, device_id_type=MESH)
+
+        gather(me - 1, 3).start()
         settle(fact, pair_sem, 1)
-        each(lambda i: pair(n - 1 - i).start(), 0, quarter, among=False)
-        each(lambda j: gather(j).start(), 0, last)
-
-    @pl.when(is_last)
-    def _():
-        pl.semaphore_wait(barrier, n - 1)
-        each(lambda j: gather(j).start(), 0, n)
+        each_odd(lambda j: pair(j - 1).start())
+        each_odd(lambda j: pair(j).start())
+        each(lambda j: pair(j).start(), 0, near, among=False)
 
     for copy in copies:
         copy.wait()
@@ -274,15 +270,34 @@
             total = term if total is None else total + term
         for j in range(n):
             part_c[j] = total[j * owned : (j + 1) * owned]
+
+        @pl.when(is_even)
+        def _():
+            settle(fact, gr_sem.at[3], 1)
+
         each(lambda j: pass_coefs(j).start(), 0, near, among=False)
         recv_c[me - pool] = part_c[me]
 
-    def make_basis(half):
+    def make_basis(half, hold=False):
         for j in range(near):
-            block = fact[half * near + j].astype(f32)
-            for i in range(rep):
-                at = i * paths + j * rows
-                spread[at : at + rows] = block
+
+            def fill(j=j):
+                block = fact[half * near + j].astype(f32)
+                for i in range(rep):
+                    at = i * paths + j * rows
+                    spread[at : at + rows] = block
+
+            if hold and j < 2:
+                pl.when(jnp.logical_not(is_final))(fill)
+
+                @pl.when(is_final)
+                def _():
+                    for i in range(rep):
+                        at = i * paths + j * rows
+                        spread[at : at + rows] = jnp.zeros((rows, spread.shape[1]), f32)
+
+            else:
+                fill()
         table = spread[...].astype(bf16)
         dims = (((1,), (1,)), ((), ()))
         loaded = lax.dot_general(split[2], table, dims, preferred_element_type=f32)
@@ -295,8 +310,8 @@
             strip = jnp.where(pair, bent[j * tall : (j + 1) * tall], 0.0).astype(bf16)
             basis[half, j * tall : (j + 1) * tall, j * width : (j + 1) * width] = strip
 
-    def half_sums(half):
-        make_basis(half)
+    def half_sums(half, hold=False):
+        make_basis(half, hold)
 
         def block_sums(right):
             cuts = [slice(c * CHUNK, (c + 1) * CHUNK) for c in range(slots // CHUNK)]
@@ -331,22 +346,29 @@
             device_id_type=MESH,
         )
 
+    for role, got in ((is_early, near - 1), (is_even, near - 2), (is_odd, near - 2)):
+        if role is is_early:
+
+            @pl.when(role)
+            def _():
+                settle(fact, gr_sem.at[0], got)
+
+        else:
+
+            @pl.when(jnp.logical_and(role, is_final))
+            def _():
+                settle(fact, gr_sem.at[1], got - 2)
+
+            @pl.when(jnp.logical_and(role, jnp.logical_not(is_final)))
+            def _():
+                settle(fact, gr_sem.at[1], got)
+
     @pl.when(is_hub)
     def _():
-        pl.semaphore_wait(barrier, n - 1)
-
-    @pl.when(is_odd)
-    def _():
-        settle(fact, gr_sem.at[1], near - 2)
-
-    @pl.when(jnp.logical_not(is_odd))
-    def _():
-        settle(fact, gr_sem.at[mine], near - 1)
-
-    @pl.when(is_hub)
-    def _():
+        pl.semaphore_wait(ready, 1)
         each(lambda i: relay(n - 1 - i).start(), 0, near, among=False)
-    half_sums(mine)
+
+    half_sums(mine, hold=True)
 
     @pl.when(is_late)
     def _():
@@ -374,19 +396,31 @@
     @pl.when(is_late)
     def _():
         make_basis(1 - mine)
+
+        @pl.when(is_final)
+        def _():
+            settle(fact, gr_sem.at[2], 2)
+            make_basis(1)
+
         settle(recv_c, cr_sem, n - pool - 1)
 
     recv[mine, me] = part[mine, me]
-    rest = recv_c[0]
-    for j in range(1, n - pool):
-        rest = rest + recv_c[j]
-    pieces = []
-    for i in range(3):
-        pieces.append(rest.astype(bf16).astype(f32))
-        rest = rest - pieces[i]
-    stack = jnp.concatenate(pieces, axis=0).astype(bf16)
-    thirds = jnp.dot(stack, basis[0], preferred_element_type=f32)
-    recv[0, pool] = thirds[2 * owned :] + thirds[owned : 2 * owned] + thirds[:owned]
+
+    def pooled(first, half):
+        rest = recv_c[first]
+        for j in range(first + 1, n - pool):
+            rest = rest + recv_c[j]
+        pieces = []
+        for i in range(3):
+            pieces.append(rest.astype(bf16).astype(f32))
+            rest = rest - pieces[i]
+        stack = jnp.concatenate(pieces, axis=0).astype(bf16)
+        thirds = jnp.dot(stack, basis[half], preferred_element_type=f32)
+        return thirds[2 * owned :] + thirds[owned : 2 * owned] + thirds[:owned]
+
+    recv[0, pool] = pooled(0, 0)
+    held_back = iota((owned, DATES * paths), 1) % paths < 2 * rows
+    recv[1, me] = recv[1, me] + jnp.where(held_back, pooled(n - 2 - pool, 1), 0.0)
     for j in range(pool + 1, n):
         recv[0, j] = jnp.zeros(recv.shape[2:], f32)
 
@@ -433,17 +467,14 @@
     def _():
         each(lambda j: settle(fact, gs_sem, near), near, n, among=False)
 
-    @pl.when(jnp.logical_or(is_even, is_odd))
-    def _():
-        settle(fact, gs_sem, last - 1)
+    @pl.when(is_even)
+    def _():
+        settle(fact, gs_sem, 1)
 
     @pl.when(is_odd)
     def _():
-        settle(fact, gs_sem, 2 * quarter)
-
-    @pl.when(is_last)
-    def _():
-        settle(fact, gs_sem, n - 1)
+        settle(fact, gs_sem, n)
+        settle(fact, gs_sem, n - 3)
 
     settle(recv.at[0], ss_sem.at[0], n - 1)
 
@@ -496,7 +527,7 @@
             pltpu.VMEM((n // 2, owned, DATES * K), f32),
             pltpu.SemaphoreType.DMA((3,)),
             pltpu.SemaphoreType.DMA,
-            pltpu.SemaphoreType.DMA((2,)),
+            pltpu.SemaphoreType.DMA((4,)),
             pltpu.SemaphoreType.DMA,
             pltpu.SemaphoreType.DMA((2,)),
             pltpu.SemaphoreType.DMA((2,)),

time: 14.2 us -> 13.8 us (0.972)
  Pallas kernels: 12.9 us -> 12.4 us
    pallas_call x1, Pallas kernels: 12.9 us -> 12.4 us  [body(): pl.pallas_call(functools.partial(kernel, n), out_shape=jax.ShapeDtypeStru...]
where the time goes in v4:
time: 13.8 us; the launch traced here: 13.7 us
  Pallas kernels  12.4 us (90%)
  between operations  0.66 us (5%)
  other arithmetic  0.56 us (4%)
    pallas_call x1, Pallas kernels, body(): pl.pallas_call(functools.partial(kernel, n), out_shape=jax.ShapeDtypeStru...  12.4 us
    div x1, other arithmetic, body(): return total / paths  0.56 us

profile of v4, /device:TPU:0, one launch (start us, length us, event | category | flops | bytes accessed | tf_op | source)
XLA Modules:
  0.0 13.7 jit_solution(14530308533447096800)
XLA Ops:
  0.7 12.4 %shard_map.91 = f32[2,8]{1,0:T(2,128)S(1)} custom-call(bf16[4,128]{1,0:T(4,128)(2,1)} %factors.1, f32[16,32]{1,0:T(8,128)} %bitcast.4, bf16[2048,256]{1,0:T(8,128)(2,1)} %trade_coef.1, s32[16,128]{1,0:T(8,128)} %bitcast.5, s32[1,2048]{1,0:T(1,128)} %bitcast.6, s32[1]{0:T(128)S(6)} %copy.10.live_count, s32[1,32]{1,0:T(1,128)} %bitcast.7, f32[2]{0:T(128)} %threshold.1, ...), custom_call_target="tpu_custom_call" | custom-call | tf_op jit(solution)/shard_map/pallas_call | solution.py:504
  13.1 0.6 %broadcast_multiply_fusion = f32[2,8]{1,0:T(2,128)} fusion(f32[2,8]{1,0:T(2,128)S(1)} %shard_map.91), kind=kLoop, calls=%fused_computation | loop fusion | flops 16 | bytes 128 | tf_op jit(solution)/shard_map/div | solution.py:552

commit v5 on v4

--- a/solution.py
+++ b/solution.py
@@ -80,8 +80,9 @@
     is_late = me >= near
     slow = near + 1
     odd = lax.rem(me, 2) == 1
-    is_even = jnp.logical_and(is_late, jnp.logical_not(odd))
+    even = jnp.logical_not(odd)
     is_odd = jnp.logical_and(is_late, odd)
+    base = mine * near
     is_final = me >= n - 2
     pool = n - recv_c.shape[0]
     is_early = jnp.logical_not(is_late)
@@ -109,13 +110,9 @@
     def greet(j):
         pl.semaphore_signal(barrier, inc=1, device_id={"trade": j}, device_id_type=MESH)
 
-    @pl.when(is_early)
-    def _():
-        each(greet, 0, near)
-
-    def each_odd(step):
+    def each_odd(step, start):
         def at(i):
-            j = near + 1 + 2 * i
+            j = start + 1 + 2 * i
 
             @pl.when(j != me)
             def _():
@@ -127,11 +124,15 @@
         else:
             lax.fori_loop(0, quarter, lambda i, c: (at(quarter - 1 - i), c)[1], 0)
 
-    @pl.when(is_odd)
+    @pl.when(odd)
     def _():
         greet(me - 1)
 
-    each_odd(greet)
+    each_odd(greet, near)
+
+    @pl.when(is_early)
+    def _():
+        each_odd(greet, 0)
 
     own = local(factors, fact.at[me], 0)
     limit_copy = local(threshold, thr_s, 1)
@@ -146,12 +147,12 @@
     copies = [local(src, dst, 2) for src, dst in pairs]
     for copy in (own, *copies, limit_copy):
         copy.start()
-    def gather(j, lane=None):
+    def gather(j):
         return pltpu.make_async_remote_copy(
             src_ref=fact.at[me],
             dst_ref=fact.at[me],
             send_sem=gs_sem,
-            recv_sem=gr_sem.at[mine if lane is None else lane],
+            recv_sem=gr_sem.at[3],
             device_id={"trade": j},
             device_id_type=MESH,
         )
@@ -166,12 +167,6 @@
             device_id_type=MESH,
         )
 
-    @pl.when(is_early)
-    def _():
-        own.wait()
-        pl.semaphore_wait(barrier, near - 1)
-        each(lambda j: gather(j).start(), 0, near)
-
     def to_partner():
         return pltpu.make_async_remote_copy(
             src_ref=factors,
@@ -188,31 +183,41 @@
             src_ref=fact.at[both],
             dst_ref=fact.at[both],
             send_sem=gs_sem,
-            recv_sem=gr_sem.at[jnp.where(jnp.logical_and(me == slow, j >= n - 2), 2, 1)],
+            recv_sem=gr_sem.at[jnp.where(jnp.logical_and(me == slow, j >= n - 2), 2, mine)],
             device_id={"trade": j},
             device_id_type=MESH,
         )
 
-    @pl.when(is_even)
+    @pl.when(even)
     def _():
         pl.semaphore_wait(barrier, 1)
         to_partner().start()
         own.wait()
 
-    @pl.when(is_odd)
+    @pl.when(odd)
     def _():
         own.wait()
-        pl.semaphore_wait(barrier, n - 1)
+
+        @pl.when(is_late)
+        def _():
+            pl.semaphore_wait(barrier, n - 1)
+
+        @pl.when(is_early)
+        def _():
+            pl.semaphore_wait(barrier, near - 1)
 
         @pl.when(me == slow)
         def _():
             pl.semaphore_signal(ready, inc=1, device_id={"trade": hub}, device_id_type=MESH)
 
-        gather(me - 1, 3).start()
+        gather(me - 1).start()
         settle(fact, pair_sem, 1)
-        each_odd(lambda j: pair(j - 1).start())
-        each_odd(lambda j: pair(j).start())
-        each(lambda j: pair(j).start(), 0, near, among=False)
+        each_odd(lambda j: pair(j - 1).start(), base)
+        each_odd(lambda j: pair(j).start(), base)
+
+        @pl.when(is_late)
+        def _():
+            each(lambda j: pair(j).start(), 0, near, among=False)
 
     for copy in copies:
         copy.wait()
@@ -271,7 +276,7 @@
         for j in range(n):
             part_c[j] = total[j * owned : (j + 1) * owned]
 
-        @pl.when(is_even)
+        @pl.when(even)
         def _():
             settle(fact, gr_sem.at[3], 1)
 
@@ -346,22 +351,17 @@
             device_id_type=MESH,
         )
 
-    for role, got in ((is_early, near - 1), (is_even, near - 2), (is_odd, near - 2)):
-        if role is is_early:
-
-            @pl.when(role)
-            def _():
-                settle(fact, gr_sem.at[0], got)
-
-        else:
-
-            @pl.when(jnp.logical_and(role, is_final))
-            def _():
-                settle(fact, gr_sem.at[1], got - 2)
-
-            @pl.when(jnp.logical_and(role, jnp.logical_not(is_final)))
-            def _():
-                settle(fact, gr_sem.at[1], got)
+    @pl.when(jnp.logical_and(is_early, even))
+    def _():
+        settle(fact, gr_sem.at[3], 1)
+
+    @pl.when(is_final)
+    def _():
+        settle(fact, gr_sem.at[1], near - 4)
+
+    @pl.when(jnp.logical_not(is_final))
+    def _():
+        settle(fact, gr_sem.at[mine], near - 2)
 
     @pl.when(is_hub)
     def _():
@@ -459,15 +459,16 @@
             result = jnp.where(column == j * rep + i, jnp.sum(own_date, axis=1, keepdims=True), result)
     out[...] = result
 
-    @pl.when(is_early)
-    def _():
-        settle(fact, gs_sem, near - 1)
+    @pl.when(jnp.logical_and(is_early, odd))
+    def _():
+        settle(fact, gs_sem, near)
+        settle(fact, gs_sem, near - 3)
 
     @pl.when(is_hub)
     def _():
         each(lambda j: settle(fact, gs_sem, near), near, n, among=False)
 
-    @pl.when(is_even)
+    @pl.when(even)
     def _():
         settle(fact, gs_sem, 1)
 

time: 13.8 us -> 13.6 us (0.986)
    pallas_call x1, Pallas kernels: 12.4 us -> 12.3 us  [body(): pl.pallas_call(functools.partial(kernel, n), out_shape=jax.ShapeDtypeStru...]
where the time goes in v5:
time: 13.6 us; the launch traced here: 13.5 us
  Pallas kernels  12.3 us (90%)
  between operations  0.66 us (5%)
  other arithmetic  0.56 us (4%)
    pallas_call x1, Pallas kernels, body(): pl.pallas_call(functools.partial(kernel, n), out_shape=jax.ShapeDtypeStru...  12.3 us
    div x1, other arithmetic, body(): return total / paths  0.56 us

profile of v5, /device:TPU:0, one launch (start us, length us, event | category | flops | bytes accessed | tf_op | source)
XLA Modules:
  0.0 13.5 jit_solution(16838536411095810629)
XLA Ops:
  0.7 12.3 %shard_map.91 = f32[2,8]{1,0:T(2,128)S(1)} custom-call(bf16[4,128]{1,0:T(4,128)(2,1)} %factors.1, f32[16,32]{1,0:T(8,128)} %bitcast.4, bf16[2048,256]{1,0:T(8,128)(2,1)} %trade_coef.1, s32[16,128]{1,0:T(8,128)} %bitcast.5, s32[1,2048]{1,0:T(1,128)} %bitcast.6, s32[1]{0:T(128)S(6)} %copy.10.live_count, s32[1,32]{1,0:T(1,128)} %bitcast.7, f32[2]{0:T(128)} %threshold.1, ...), custom_call_target="tpu_custom_call" | custom-call | tf_op jit(solution)/shard_map/pallas_call | solution.py:505
  12.9 0.6 %broadcast_multiply_fusion = f32[2,8]{1,0:T(2,128)} fusion(f32[2,8]{1,0:T(2,128)S(1)} %shard_map.91), kind=kLoop, calls=%fused_computation | loop fusion | flops 16 | bytes 128 | tf_op jit(solution)/shard_map/div | solution.py:553

commit v6 on v5

--- a/solution.py
+++ b/solution.py
@@ -12,7 +12,7 @@
 DATES = 8
 LAG = 2
 LANES = 128
-CHUNK = 256
+CHUNK = 128
 COLS = 512
 MESH = pl.DeviceIdType.MESH
 f32 = jnp.float32

time: 13.6 us -> 13.6 us (level)
  no operation moved by 1% of the time
where the time goes in v6:
time: 13.6 us; the launch traced here: 13.5 us
  Pallas kernels  12.2 us (90%)
  between operations  0.66 us (5%)
  other arithmetic  0.56 us (4%)
    pallas_call x1, Pallas kernels, body(): pl.pallas_call(functools.partial(kernel, n), out_shape=jax.ShapeDtypeStru...  12.2 us
    div x1, other arithmetic, body(): return total / paths  0.56 us

profile of v6, /device:TPU:0, one launch (start us, length us, event | category | flops | bytes accessed | tf_op | source)
XLA Modules:
  0.0 13.5 jit_solution(11101210666094465629)
XLA Ops:
  0.7 12.2 %shard_map.91 = f32[2,8]{1,0:T(2,128)S(1)} custom-call(bf16[4,128]{1,0:T(4,128)(2,1)} %factors.1, f32[16,32]{1,0:T(8,128)} %bitcast.4, bf16[2048,256]{1,0:T(8,128)(2,1)} %trade_coef.1, s32[16,128]{1,0:T(8,128)} %bitcast.5, s32[1,2048]{1,0:T(1,128)} %bitcast.6, s32[1]{0:T(128)S(6)} %copy.10.live_count, s32[1,32]{1,0:T(1,128)} %bitcast.7, f32[2]{0:T(128)} %threshold.1, ...), custom_call_target="tpu_custom_call" | custom-call | tf_op jit(solution)/shard_map/pallas_call | solution.py:505
  12.9 0.6 %broadcast_multiply_fusion = f32[2,8]{1,0:T(2,128)} fusion(f32[2,8]{1,0:T(2,128)S(1)} %shard_map.91), kind=kLoop, calls=%fused_computation | loop fusion | flops 16 | bytes 128 | tf_op jit(solution)/shard_map/div | solution.py:553

commit v7 on v5

--- a/solution.py
+++ b/solution.py
@@ -79,6 +79,7 @@
     is_hub = me == hub
     is_late = me >= near
     slow = near + 1
+    helper = near + 3
     odd = lax.rem(me, 2) == 1
     even = jnp.logical_not(odd)
     is_odd = jnp.logical_and(is_late, odd)
@@ -128,7 +129,12 @@
     def _():
         greet(me - 1)
 
-    each_odd(greet, near)
+    def greet_late(j):
+        @pl.when(jnp.logical_not(jnp.logical_and(is_final, j == slow)))
+        def _():
+            greet(j)
+
+    each_odd(greet_late, near)
 
     @pl.when(is_early)
     def _():
@@ -183,7 +189,7 @@
             src_ref=fact.at[both],
             dst_ref=fact.at[both],
             send_sem=gs_sem,
-            recv_sem=gr_sem.at[jnp.where(jnp.logical_and(me == slow, j >= n - 2), 2, mine)],
+            recv_sem=gr_sem.at[mine],
             device_id={"trade": j},
             device_id_type=MESH,
         )
@@ -198,40 +204,48 @@
     def _():
         own.wait()
 
-        @pl.when(is_late)
+        @pl.when(jnp.logical_and(is_late, me != slow))
         def _():
             pl.semaphore_wait(barrier, n - 1)
 
+        @pl.when(me == slow)
+        def _():
+            pl.semaphore_wait(barrier, n - 3)
+
         @pl.when(is_early)
         def _():
             pl.semaphore_wait(barrier, near - 1)
 
-        @pl.when(me == slow)
+        @pl.when(me == helper)
         def _():
             pl.semaphore_signal(ready, inc=1, device_id={"trade": hub}, device_id_type=MESH)
 
         gather(me - 1).start()
         settle(fact, pair_sem, 1)
-        each_odd(lambda j: pair(j - 1).start(), base)
-        each_odd(lambda j: pair(j).start(), base)
 
         @pl.when(is_late)
         def _():
             each(lambda j: pair(j).start(), 0, near, among=False)
+
+        def pass_on(j):
+            @pl.when(jnp.logical_not(jnp.logical_and(me == slow, j >= n - 2)))
+            def _():
+                pair(j).start()
+
+        each_odd(lambda j: pass_on(j - 1), base)
+        each_odd(pass_on, base)
 
     for copy in copies:
         copy.wait()
     limit_copy.wait()
     tiled = (iota((F, LANES), 1) % F == iota((F, LANES), 0)).astype(f32).astype(bf16)
-    diag = iota((DATES * K, LANES), 0) // K == iota((DATES * K, LANES), 1) // F
-    rest = load_v[...]
+    diag = iota((LANES, DATES * K), 0) // F == iota((LANES, DATES * K), 1) // K
+    rest = jnp.concatenate([load_v[...]] * DATES, axis=1)
     for i in range(3):
         piece = rest.astype(bf16)
         rest = rest - piece.astype(f32)
-        wide = lax.dot_general(piece, tiled, (((0,), (0,)), ((), ())), preferred_element_type=f32)
-        wide = jnp.concatenate([wide] * DATES, axis=0)
-        split[i] = jnp.where(diag, wide, 0.0).astype(bf16)
-    basis[...] = jnp.zeros(basis.shape, bf16)
+        wide = lax.dot_general(tiled, piece, (((0,), (0,)), ((), ())), preferred_element_type=f32)
+        split[i * LANES : (i + 1) * LANES] = jnp.where(diag, wide, 0.0).astype(bf16)
 
     found = nrow_v[...] == iota((sets, sets), 0)
     owner_set = jnp.sum(jnp.where(found, iota((sets, sets), 1), 0).astype(f32), axis=1, keepdims=True)
@@ -288,39 +302,33 @@
 
             def fill(j=j):
                 block = fact[half * near + j].astype(f32)
-                for i in range(rep):
-                    at = i * paths + j * rows
-                    spread[at : at + rows] = block
+                spread[j * rows : (j + 1) * rows] = block
 
             if hold and j < 2:
                 pl.when(jnp.logical_not(is_final))(fill)
 
                 @pl.when(is_final)
                 def _():
-                    for i in range(rep):
-                        at = i * paths + j * rows
-                        spread[at : at + rows] = jnp.zeros((rows, spread.shape[1]), f32)
+                    spread[j * rows : (j + 1) * rows] = jnp.zeros((rows, spread.shape[1]), f32)
 
             else:
                 fill()
-        table = spread[...].astype(bf16)
-        dims = (((1,), (1,)), ((), ()))
-        loaded = lax.dot_general(split[2], table, dims, preferred_element_type=f32)
-        loaded += lax.dot_general(split[1], table, dims, preferred_element_type=f32)
-        loaded += lax.dot_general(split[0], table, dims, preferred_element_type=f32)
-        bent = jnp.tanh(loaded)
-        tall = rep * K
-        pair = iota((tall, width), 0) // K == iota((tall, width), 1) // paths
-        for j in range(DATES // rep):
-            strip = jnp.where(pair, bent[j * tall : (j + 1) * tall], 0.0).astype(bf16)
-            basis[half, j * tall : (j + 1) * tall, j * width : (j + 1) * width] = strip
+        table = jnp.concatenate([spread[...].astype(bf16)] * 3, axis=1)
+        bent = jnp.tanh(jnp.dot(table, split[...], preferred_element_type=f32))
+        date = iota(bent.shape, 1) // K
+        for d in range(DATES):
+            basis[half, d * paths : (d + 1) * paths] = jnp.where(date == d, bent, 0.0).astype(bf16)
 
     def half_sums(half, hold=False):
         make_basis(half, hold)
 
+        across = (((1,), (1,)), ((), ()))
+
         def block_sums(right):
             cuts = [slice(c * CHUNK, (c + 1) * CHUNK) for c in range(slots // CHUNK)]
-            values = [jnp.dot(coef_v[cut], right, preferred_element_type=f32).astype(bf16) for cut in cuts]
+            values = [
+                lax.dot_general(coef_v[cut], right, across, preferred_element_type=f32).astype(bf16) for cut in cuts
+            ]
             total = None
             for cut, value in zip(cuts, values):
                 term = jnp.dot(onehot[:, cut], value, preferred_element_type=f32)
@@ -334,7 +342,7 @@
 
             def one(b, carry):
                 side = pl.ds(pl.multiple_of(b * COLS, COLS), COLS)
-                acc[:, side] = block_sums(basis[half, :, side])
+                acc[:, side] = block_sums(basis[half, side])
                 return carry
 
             lax.fori_loop(0, blocks, one, 0)
@@ -363,6 +371,22 @@
     def _():
         settle(fact, gr_sem.at[mine], near - 2)
 
+    def late_pair(j):
+        held = pl.ds(near, 2)
+        return pltpu.make_async_remote_copy(
+            src_ref=fact.at[held],
+            dst_ref=fact.at[held],
+            send_sem=gs_sem,
+            recv_sem=gr_sem.at[2],
+            device_id={"trade": j},
+            device_id_type=MESH,
+        )
+
+    @pl.when(me == helper)
+    def _():
+        late_pair(n - 2).start()
+        late_pair(n - 1).start()
+
     @pl.when(is_hub)
     def _():
         pl.semaphore_wait(ready, 1)
@@ -415,7 +439,7 @@
             pieces.append(rest.astype(bf16).astype(f32))
             rest = rest - pieces[i]
         stack = jnp.concatenate(pieces, axis=0).astype(bf16)
-        thirds = jnp.dot(stack, basis[half], preferred_element_type=f32)
+        thirds = lax.dot_general(stack, basis[half], (((1,), (1,)), ((), ())), preferred_element_type=f32)
         return thirds[2 * owned :] + thirds[owned : 2 * owned] + thirds[:owned]
 
     recv[0, pool] = pooled(0, 0)
@@ -475,7 +499,15 @@
     @pl.when(is_odd)
     def _():
         settle(fact, gs_sem, n)
-        settle(fact, gs_sem, n - 3)
+        settle(fact, gs_sem, n - 7)
+
+        @pl.when(me != slow)
+        def _():
+            settle(fact, gs_sem, 4)
+
+        @pl.when(me == helper)
+        def _():
+            settle(fact, gs_sem, 4)
 
     settle(recv.at[0], ss_sem.at[0], n - 1)
 
@@ -516,10 +548,10 @@
             pltpu.VMEM((1, sets), jnp.int32),
             pltpu.SMEM((owned,), f32),
             pltpu.VMEM((owned, paths), f32),
-            pltpu.VMEM((3, DATES * K, DATES * F), bf16),
+            pltpu.VMEM((3 * DATES * F, DATES * K), bf16),
             pltpu.VMEM((sets, slots), bf16),
-            pltpu.VMEM((rep * half, DATES * F), f32),
-            pltpu.VMEM((2, DATES * K, wide), bf16),
+            pltpu.VMEM((half, DATES * F), f32),
+            pltpu.VMEM((2, wide, DATES * K), bf16),
             pltpu.VMEM((2, owned, LAG * half), f32),
             pltpu.VMEM((sets, wide), f32),
             pltpu.VMEM((2, n, owned, wide), f32),

time: 13.6 us -> 13.5 us (level)
  Pallas kernels: 12.3 us -> 12.1 us
    pallas_call x1, Pallas kernels: 12.3 us -> 12.1 us  [body(): pl.pallas_call(functools.partial(kernel, n), out_shape=jax.ShapeDtypeStru...]
where the time goes in v7:
time: 13.5 us; the launch traced here: 13.3 us
  Pallas kernels  12.1 us (90%)
  between operations  0.66 us (5%)
  other arithmetic  0.56 us (4%)
    pallas_call x1, Pallas kernels, body(): pl.pallas_call(functools.partial(kernel, n), out_shape=jax.ShapeDtypeStru...  12.1 us
    div x1, other arithmetic, body(): return total / paths  0.56 us

profile of v7, /device:TPU:0, one launch (start us, length us, event | category | flops | bytes accessed | tf_op | source)
XLA Modules:
  0.0 13.3 jit_solution(13699183075158770547)
XLA Ops:
  0.7 12.1 %shard_map.91 = f32[2,8]{1,0:T(2,128)S(1)} custom-call(bf16[4,128]{1,0:T(4,128)(2,1)} %factors.1, f32[16,32]{1,0:T(8,128)} %bitcast.4, bf16[2048,256]{1,0:T(8,128)(2,1)} %trade_coef.1, s32[16,128]{1,0:T(8,128)} %bitcast.5, s32[1,2048]{1,0:T(1,128)} %bitcast.6, s32[1]{0:T(128)S(6)} %copy.10.live_count, s32[1,32]{1,0:T(1,128)} %bitcast.7, f32[2]{0:T(128)} %threshold.1, ...), custom_call_target="tpu_custom_call" | custom-call | tf_op jit(solution)/shard_map/pallas_call | solution.py:537
  12.7 0.6 %broadcast_multiply_fusion = f32[2,8]{1,0:T(2,128)} fusion(f32[2,8]{1,0:T(2,128)S(1)} %shard_map.91), kind=kLoop, calls=%fused_computation | loop fusion | flops 16 | bytes 128 | tf_op jit(solution)/shard_map/div | solution.py:585
